TPU v7x, 32 devices: a whole 2x2x4 slice. The times are simulated.
32 devices in a mesh: row: 8 (over y, x, core), col: 4 (over z).
Axes of the slice: x: 2, y: 2, z: 4, core: 2. Of those that a mesh axis runs over, the one named last changes fastest.
Arguments:
- coeffs: bfloat16 [6144, 4096], P('row', 'col'), may hold values from -0.00390625 to 0.00390625
- occupation: float32 [4096], P('col'), may hold values from 0.5 to 2
- basis_on_grid: bfloat16 [320, 512, 512], P('row'), may hold values from -6 to 6
- basis_map: int32 [320, 512], P('row'), may hold values from 0 to 6143, as said below
- basis_count: int32 [320], P('row'), may hold values from 256 to 512
- batch_atom: int32 [320], P('row'), may hold values from 0 to 63
- harmonics: float32 [320, 49, 512], P('row'), may hold values from -0.25 to 0.25
Outputs:
- density: float32 [320, 512], P('row', 'col')
- moments: float32 [64, 49], replicated
Inputs may be any that keep to these rules, and one draw needn't show every extreme that they name: `basis_map`: the slots of one batch name distinct basis functions. With R = 768 and o = b // 40, batch b names only basis functions q * R + (o * 96 + w) mod R with 0 <= q < 8 and 0 <= w < 96.
All inputs are finite; a program needn't handle non-finite values.
Results may differ from a plain program's by a relative error of at most 0.0003.
Values may be sent and summed in bfloat16 or wider, within the bound.
No kernel may reach another device: no remote copies, remote signals or barrier semaphores. Data moves between devices by JAX's collectives and lax.ppermute only.
A program may use at most 192 MiB of HBM per device.

v0:
```python
import jax
import jax.numpy as jnp
from jax import lax
from jax.sharding import PartitionSpec as P

WIN = 96
NATOM = 64


def shards(coeffs, occupation, basis_on_grid, basis_map, basis_count, batch_atom, harmonics):
    batches, points, slots = basis_on_grid.shape
    owned = coeffs.shape[0]
    owners = lax.axis_size("row")
    target = lax.broadcasted_iota(jnp.int32, (owners, WIN), 0)
    offset = lax.broadcasted_iota(jnp.int32, (owners, WIN), 1)
    outgoing_ids = jnp.mod(target * WIN + offset, owned).reshape(-1)
    outgoing = jnp.take(coeffs, outgoing_ids, axis=0)
    window = lax.all_to_all(outgoing, "row", split_axis=0, concat_axis=0, tiled=True)
    start = jnp.mod(lax.axis_index("row") * WIN, owned)
    source = basis_map // owned
    within = jnp.mod(basis_map % owned - start, owned)
    local_ids = source * WIN + within
    selected = jnp.take(window, local_ids, axis=0)
    slot_ids = lax.broadcasted_iota(jnp.int32, (batches, slots), 1)
    keep = slot_ids < basis_count[:, None]
    masked = jnp.where(keep[:, None, :], basis_on_grid, jnp.zeros_like(basis_on_grid))
    orbital = jnp.einsum("bps,bsk->bpk", masked, selected, preferred_element_type=jnp.float32)
    partial_density = jnp.sum(orbital * orbital * occupation[None, None, :], axis=2)
    atom_ids = lax.broadcasted_iota(jnp.int32, (batches, NATOM), 1)
    member = (batch_atom[:, None] == atom_ids).astype(jnp.float32)
    full_density = lax.psum(partial_density, "col")
    local_moment = jnp.einsum(
        "blp,bp->bl", harmonics, full_density, precision=lax.Precision.HIGHEST
    )
    atom_part = jnp.dot(member.T, local_moment, precision=lax.Precision.HIGHEST)
    moments = lax.psum(atom_part, "row")
    share = points // lax.axis_size("col")
    density = lax.dynamic_slice_in_dim(full_density, lax.axis_index("col") * share, share, 1)
    return (density, moments)


def solution(mesh):
    placed = (
        P("row", "col"),
        P("col"),
        P("row", None, None),
        P("row", None),
        P("row"),
        P("row"),
        P("row", None, None),
    )
    return jax.shard_map(
        shards, mesh=mesh, in_specs=placed, out_specs=(P("row", "col"), P()), check_vma=False
    )
```

profile of v0, /device:TPU:0, one launch (start us, length us, event | category | flops | bytes accessed | tf_op | source)
XLA Modules:
  0.0 228.4 jit_solution(9429908495071229577)
XLA Ops:
  7.2 0.0 copy-start
  7.2 0.1 add_remainder_fusion
  7.3 0.1 compare_and_fusion.1
  7.4 0.1 rem.52
  7.5 1.1 copy-done
  8.6 2.8 %gather_fusion = bf16[768,1024]{1,0:T(8,128)(2,1)S(1)} fusion(bf16[768,1024]{1,0:T(8,128)(2,1)S(1)} %copy-done, s32[1024]{0:T(1024)S(1)} %pad_clamp_fusion), kind=kCustom, calls=%fused_computation | custom fusion | bytes 3148800 | tf_op jit(solution)/shard_map/jit(_take)/gather | solution.py:17
  11.4 1.4 broadcast_select_fusion
  12.8 5.2 %all-to-all-start = ((bf16[8,96,1024]{2,1,0:T(8,128)(2,1)}), bf16[8,96,1024]{2,1,0:T(8,128)(2,1)S(1)}, u32[]{:S(2)}, u32[]{:S(2)}) async-start(bf16[8,96,1024]{2,1,0:T(8,128)(2,1)} %broadcast_select_fusion), calls=%async_computation | async-start | bytes 3145728 | tf_op jit(solution)/shard_map/all_to_all | solution.py:18
  18.0 0.0 all-reduce.2.cloned.1.call-start
  18.0 1.0 compare_and_fusion
  19.1 0.7 iota_compare_fusion
  19.9 19.1 %all-to-all-done = bf16[8,96,1024]{2,1,0:T(8,128)(2,1)S(1)} async-done(((bf16[8,96,1024]{2,1,0:T(8,128)(2,1)}), bf16[8,96,1024]{2,1,0:T(8,128)(2,1)S(1)}, u32[]{:S(2)}, u32[]{:S(2)}) %all-to-all-start) | async-done | bytes 1572896 | tf_op jit(solution)/shard_map/all_to_all | solution.py:18
  39.0 0.0 copy-start.2
  39.0 87.0 %gather_fusion.1 = bf16[20480,1024]{1,0:T(8,128)(2,1)} fusion(bf16[768,1024]{1,0:T(8,128)(2,1)S(1)} %bitcast.9, s32[20480]{0:T(1024)S(1)} %broadcast_clamp_fusion), kind=kCustom, calls=%fused_computation.1 | custom fusion | bytes 83968000 | tf_op jit(solution)/shard_map/jit(_take)/gather | solution.py:23
  125.9 0.0 copy-done.2
  125.9 0.0 copy-start.3
  125.9 0.0 copy-start.1
  125.9 29.3 %multiply_reduce_fusion = f32[40,512]{1,0:T(8,128)} fusion(f32[1024]{0:T(1024)S(1)} %copy-done.2, bf16[40,512,1024]{2,1,0:T(8,128)(2,1)} %bitcast.10, pred[40,512]{1,0:T(8,128)(4,1)S(1)} %get-tuple-element.2, bf16[40,512,512]{2,1,0:T(8,128)(2,1)} %param.9, pred[40,512]{1,0:T(8,128)(4,1)S(1)} %iota_compare_fusion), kind=kOutput, calls=%fused_computation.2 | convolution fusion | flops 21569187840 | bytes 63041536 | tf_op jit(solution)/shard_map/bps,bsk->bpk/dot_general | solution.py:27
  155.2 0.0 all-reduce.2.cloned.1.call-update
  155.3 33.8 %all-reduce.2.cloned.1.call-done = f32[40,512]{1,0:T(8,128)} async-done(((f32[40,512]{1,0:T(8,128)}), f32[40,512]{1,0:T(8,128)}) %all-reduce.2.cloned.1.call-update) | async-done | bytes 81936 | tf_op jit(solution)/shard_map/psum | solution.py:31
  189.0 7.9 %fusion.11 = f32[40,1,49]{2,1,0:T(1,128)S(1)} fusion(f32[40,49,512]{2,0,1:T(8,128)} %param.13, f32[40,512,1]{1,0,2:T(8,128)} %bitcast.14), kind=kOutput, calls=%fused_computation.10 | convolution fusion | flops 12042240 | bytes 4103840 | tf_op jit(solution)/shard_map/blp,bp->bl/dot_general | solution.py:32
  196.9 0.0 copy-done.3
  196.9 0.2 fusion.19
  197.2 23.0 %psum.15 = f32[64,49]{0,1:T(8,128)} all-reduce(f32[64,49]{0,1:T(8,128)S(1)} %fusion.19), channel_id=1, replica_groups=mesh['row'=8,'col'=4] {'row'}, use_global_device_ids=true, to_apply=%region_2.3 | all-reduce | flops 3136 | bytes 25088 | tf_op jit(solution)/shard_map/psum | solution.py:36
  220.2 1.3 constant_dynamic-slice_fusion
  221.5 0.0 copy-done.1
  (5 shorter events, 0.1 us)
Async XLA Ops:
  7.2 1.4 copy-start
  12.8 26.2 %all-to-all-start = ((bf16[8,96,1024]{2,1,0:T(8,128)(2,1)}), bf16[8,96,1024]{2,1,0:T(8,128)(2,1)S(1)}, u32[]{:S(2)}, u32[]{:S(2)}) async-start(bf16[8,96,1024]{2,1,0:T(8,128)(2,1)} %broadcast_select_fusion), calls=%async_computation | async-start | bytes 3145728 | tf_op jit(solution)/shard_map/all_to_all | solution.py:18
  18.0 171.1 %all-reduce.2.cloned.1.call-start = ((), (), s32[]{:S(2)}) async-start(), calls=%async_computation.1 | async-start | bytes 163840 | tf_op jit(solution)/shard_map/psum | solution.py:31
  39.0 87.0 %copy-start.2 = (f32[1024]{0:T(1024)S(1)}, f32[1024]{0:T(1024)}, u32[]{:S(2)}) copy-start(f32[1024]{0:T(1024)} %param.8) | copy-start | bytes 12292
  125.9 71.0 %copy-start.3 = (s32[40]{0:T(128)S(1)}, s32[40]{0:T(128)}, u32[]{:S(2)}) copy-start(s32[40]{0:T(128)} %param.12) | copy-start | bytes 484
  125.9 95.6 %copy-start.1 = (bf16[768,1024]{1,0:T(8,128)(2,1)S(1)}, bf16[768,1024]{1,0:T(8,128)(2,1)}, u32[]{:S(2)}) copy-start(bf16[768,1024]{1,0:T(8,128)(2,1)} %param.7) | copy-start | bytes 4718596
Sparse Core Ops, SparseCore 0:
  155.4 33.6 all-reduce.1
where the time goes:
time: 229 us; the launch traced here: 228 us
  local copies, waits for them, and re-layouts  92.3 us (40%)
  waiting for transfers between devices  52.9 us (23%)
  matrix products  37.5 us (16%)
  blocking collectives  23 us (10%)
  between operations  14.1 us (6%)
  starting transfers between devices  5.24 us (2%)
  other arithmetic  3.37 us (1%)
    gather x1, local copies, waits for them, and re-layouts, shards(): selected = jnp.take(window, local_ids, axis=0)  87 us
    psum x1, waiting for transfers between devices, shards(): full_density = lax.psum(partial_density, 'col')  33.8 us
    dot_general x1, matrix products, shards(): jnp.einsum('bps,bsk->bpk', masked, selected, preferred_element_type=jnp.f...  29.3 us
    psum x1, blocking collectives, shards(): moments = lax.psum(atom_part, 'row')  23 us
    all_to_all x1, waiting for transfers between devices, shards(): lax.all_to_all(outgoing, 'row', split_axis=0, concat_axis=0, tiled=True)  19.1 us
    dot_general x1, matrix products, shards(): jnp.einsum('blp,bp->bl', harmonics, full_density, precision=lax.Precision...  7.89 us
    all_to_all x1, starting transfers between devices, shards(): lax.all_to_all(outgoing, 'row', split_axis=0, concat_axis=0, tiled=True)  5.2 us
  transfers between devices with their start and end apart: 2, of which 2 were waited for; matrix products, arithmetic and copies ran while one was open for 1% of the time, Pallas kernels for 0%

commit v1 on v0

--- a/solution.py
+++ b/solution.py
@@ -28,7 +28,7 @@
     partial_density = jnp.sum(orbital * orbital * occupation[None, None, :], axis=2)
     atom_ids = lax.broadcasted_iota(jnp.int32, (batches, NATOM), 1)
     member = (batch_atom[:, None] == atom_ids).astype(jnp.float32)
-    full_density = lax.psum(partial_density, "col")
+    full_density = jnp.sum(lax.all_gather(partial_density, "col"), axis=0)
     local_moment = jnp.einsum(
         "blp,bp->bl", harmonics, full_density, precision=lax.Precision.HIGHEST
     )

time: 229 us -> 195 us (0.85)
  waiting for transfers between devices: 52.9 us -> 19.1 us
  blocking collectives: 23 us -> 38 us
  between operations: 14.1 us -> 0.72 us
    psum x1 -> x0, waiting for transfers between devices: 33.8 us -> none  [shards(): full_density = lax.psum(partial_density, 'col')]
    all_gather x0 -> x1, blocking collectives: none -> 15 us  [shards(): full_density = jnp.sum(lax.all_gather(partial_density, 'col'), axis=0)]
  transfers between devices with their start and end apart: 2 -> 1, of which waited for: 2 -> 1; matrix products, arithmetic and copies ran while one was open for 1% -> 1% of each run, Pallas kernels for 0% -> 0%
where the time goes in v1:
time: 195 us
  local copies, waits for them, and re-layouts  91.6 us (47%)
  blocking collectives  38 us (19%)
  matrix products  36.8 us (19%)
  waiting for transfers between devices  19.1 us (10%)
  starting transfers between devices  5.2 us (3%)
  other arithmetic  3.39 us (2%)
    gather x1, local copies, waits for them, and re-layouts, shards(): selected = jnp.take(window, local_ids, axis=0)  87 us
    dot_general x1, matrix products, shards(): jnp.einsum('bps,bsk->bpk', masked, selected, preferred_element_type=jnp.f...  28.7 us
    psum x1, blocking collectives, shards(): moments = lax.psum(atom_part, 'row')  23 us
    all_to_all x1, waiting for transfers between devices, shards(): lax.all_to_all(outgoing, 'row', split_axis=0, concat_axis=0, tiled=True)  19.1 us
    all_gather x1, blocking collectives, shards(): full_density = jnp.sum(lax.all_gather(partial_density, 'col'), axis=0)  15 us
    dot_general x1, matrix products, shards(): jnp.einsum('blp,bp->bl', harmonics, full_density, precision=lax.Precision...  7.84 us
    all_to_all x1, starting transfers between devices, shards(): lax.all_to_all(outgoing, 'row', split_axis=0, concat_axis=0, tiled=True)  5.2 us
  transfers between devices with their start and end apart: 1, of which 1 were waited for; matrix products, arithmetic and copies ran while one was open for 1% of the time, Pallas kernels for 0%

profile of v1, /device:TPU:0, one launch (start us, length us, event | category | flops | bytes accessed | tf_op | source)
XLA Modules:
  0.0 194.8 jit_solution(12261363362341990561)
XLA Ops:
  0.6 0.0 copy-start
  0.7 0.1 add_remainder_fusion
  0.7 0.1 compare_and_fusion.1
  0.8 0.1 rem.52
  0.9 1.1 copy-done
  2.0 2.8 %gather_fusion = bf16[768,1024]{1,0:T(8,128)(2,1)S(1)} fusion(bf16[768,1024]{1,0:T(8,128)(2,1)S(1)} %copy-done, s32[1024]{0:T(1024)S(1)} %pad_clamp_fusion), kind=kCustom, calls=%fused_computation | custom fusion | bytes 3148800 | tf_op jit(solution)/shard_map/jit(_take)/gather | solution.py:17
  4.9 1.4 broadcast_select_fusion
  6.2 5.2 %all-to-all-start = ((bf16[8,96,1024]{2,1,0:T(8,128)(2,1)}), bf16[8,96,1024]{2,1,0:T(8,128)(2,1)S(1)}, u32[]{:S(2)}, u32[]{:S(2)}) async-start(bf16[8,96,1024]{2,1,0:T(8,128)(2,1)} %broadcast_select_fusion), calls=%async_computation | async-start | bytes 3145728 | tf_op jit(solution)/shard_map/all_to_all | solution.py:18
  11.4 1.0 compare_and_fusion
  12.5 0.7 iota_compare_fusion
  13.3 19.1 %all-to-all-done = bf16[8,96,1024]{2,1,0:T(8,128)(2,1)S(1)} async-done(((bf16[8,96,1024]{2,1,0:T(8,128)(2,1)}), bf16[8,96,1024]{2,1,0:T(8,128)(2,1)S(1)}, u32[]{:S(2)}, u32[]{:S(2)}) %all-to-all-start) | async-done | bytes 1572896 | tf_op jit(solution)/shard_map/all_to_all | solution.py:18
  32.4 0.0 copy-start.2
  32.4 87.0 %gather_fusion.1 = bf16[20480,1024]{1,0:T(8,128)(2,1)} fusion(bf16[768,1024]{1,0:T(8,128)(2,1)S(1)} %bitcast.10, s32[20480]{0:T(1024)S(1)} %broadcast_clamp_fusion), kind=kCustom, calls=%fused_computation.1 | custom fusion | bytes 83968000 | tf_op jit(solution)/shard_map/jit(_take)/gather | solution.py:23
  119.4 0.0 copy-done.2
  119.4 0.0 copy-start.3
  119.4 0.0 copy-start.1
  119.4 28.7 %multiply_reduce_fusion = f32[40,512]{1,0:T(8,128)S(1)} fusion(f32[1024]{0:T(1024)S(1)} %copy-done.2, bf16[40,512,1024]{2,1,0:T(8,128)(2,1)} %bitcast.11, pred[40,512]{1,0:T(8,128)(4,1)S(1)} %get-tuple-element.2, bf16[40,512,512]{2,1,0:T(8,128)(2,1)} %param.9, pred[40,512]{1,0:T(8,128)(4,1)S(1)} %iota_compare_fusion), kind=kOutput, calls=%fused_computation.2 | convolution fusion | flops 21569187840 | bytes 63041536 | tf_op jit(solution)/shard_map/bps,bsk->bpk/dot_general | solution.py:27
  148.1 15.0 %all-gather = f32[160,512]{1,0:T(8,128)S(1)} all-gather(f32[40,512]{1,0:T(8,128)S(1)} %multiply_reduce_fusion), channel_id=2, replica_groups=mesh['row'=8,'col'=4] {'col'}, dimensions={0}, use_global_device_ids=true | all-gather | bytes 409600 | tf_op jit(solution)/shard_map/all_gather | solution.py:31
  163.1 0.6 constant_dynamic-slice_fusion
  163.8 7.8 %fusion.11 = f32[40,1,49]{2,1,0:T(1,128)S(1)} fusion(f32[40,49,512]{2,0,1:T(8,128)} %param.13, f32[40,512,1]{1,0,2:T(8,128)S(1)} %bitcast.14), kind=kOutput, calls=%fused_computation.10 | convolution fusion | flops 12042240 | bytes 4103840 | tf_op jit(solution)/shard_map/blp,bp->bl/dot_general | solution.py:32
  171.6 0.0 copy-done.3
  171.6 0.2 fusion.19
  171.8 23.0 %psum.7 = f32[64,49]{0,1:T(8,128)} all-reduce(f32[64,49]{0,1:T(8,128)S(1)} %fusion.19), channel_id=1, replica_groups=mesh['row'=8,'col'=4] {'row'}, use_global_device_ids=true, to_apply=%region_2.3 | all-reduce | flops 3136 | bytes 25088 | tf_op jit(solution)/shard_map/psum | solution.py:36
  194.8 0.0 copy-done.1
  (6 shorter events, 0.1 us)
Async XLA Ops:
  0.6 1.4 copy-start
  6.2 26.2 %all-to-all-start = ((bf16[8,96,1024]{2,1,0:T(8,128)(2,1)}), bf16[8,96,1024]{2,1,0:T(8,128)(2,1)S(1)}, u32[]{:S(2)}, u32[]{:S(2)}) async-start(bf16[8,96,1024]{2,1,0:T(8,128)(2,1)} %broadcast_select_fusion), calls=%async_computation | async-start | bytes 3145728 | tf_op jit(solution)/shard_map/all_to_all | solution.py:18
  32.4 87.0 %copy-start.2 = (f32[1024]{0:T(1024)S(1)}, f32[1024]{0:T(1024)}, u32[]{:S(2)}) copy-start(f32[1024]{0:T(1024)} %param.8) | copy-start | bytes 12292
  119.4 52.2 %copy-start.3 = (s32[40]{0:T(128)S(1)}, s32[40]{0:T(128)}, u32[]{:S(2)}) copy-start(s32[40]{0:T(128)} %param.12) | copy-start | bytes 484
  119.4 75.5 %copy-start.1 = (bf16[768,1024]{1,0:T(8,128)(2,1)S(1)}, bf16[768,1024]{1,0:T(8,128)(2,1)}, u32[]{:S(2)}) copy-start(bf16[768,1024]{1,0:T(8,128)(2,1)} %param.7) | copy-start | bytes 4718596

commit v2 on v0

--- a/solution.py
+++ b/solution.py
@@ -33,7 +33,7 @@
         "blp,bp->bl", harmonics, full_density, precision=lax.Precision.HIGHEST
     )
     atom_part = jnp.dot(member.T, local_moment, precision=lax.Precision.HIGHEST)
-    moments = lax.psum(atom_part, "row")
+    moments = jnp.sum(lax.all_gather(atom_part, "row"), axis=0)
     share = points // lax.axis_size("col")
     density = lax.dynamic_slice_in_dim(full_density, lax.axis_index("col") * share, share, 1)
     return (density, moments)

time: 229 us -> 216 us (0.943)
  blocking collectives: 23 us -> 9.26 us
    psum x1 -> x0, blocking collectives: 23 us -> none  [shards(): moments = lax.psum(atom_part, 'row')]
    all_gather x0 -> x1, blocking collectives: none -> 9.26 us  [shards(): moments = jnp.sum(lax.all_gather(atom_part, 'row'), axis=0)]
where the time goes in v2:
time: 216 us; the launch traced here: 215 us
  local copies, waits for them, and re-layouts  92.3 us (43%)
  waiting for transfers between devices  52.9 us (24%)
  matrix products  37.5 us (17%)
  between operations  14.1 us (7%)
  blocking collectives  9.26 us (4%)
  starting transfers between devices  5.24 us (2%)
  other arithmetic  4 us (2%)
    gather x1, local copies, waits for them, and re-layouts, shards(): selected = jnp.take(window, local_ids, axis=0)  87 us
    psum x1, waiting for transfers between devices, shards(): full_density = lax.psum(partial_density, 'col')  33.8 us
    dot_general x1, matrix products, shards(): jnp.einsum('bps,bsk->bpk', masked, selected, preferred_element_type=jnp.f...  29.3 us
    all_to_all x1, waiting for transfers between devices, shards(): lax.all_to_all(outgoing, 'row', split_axis=0, concat_axis=0, tiled=True)  19.1 us
    all_gather x1, blocking collectives, shards(): moments = jnp.sum(lax.all_gather(atom_part, 'row'), axis=0)  9.26 us
    dot_general x1, matrix products, shards(): jnp.einsum('blp,bp->bl', harmonics, full_density, precision=lax.Precision...  7.89 us
    all_to_all x1, starting transfers between devices, shards(): lax.all_to_all(outgoing, 'row', split_axis=0, concat_axis=0, tiled=True)  5.2 us
  transfers between devices with their start and end apart: 2, of which 2 were waited for; matrix products, arithmetic and copies ran while one was open for 1% of the time, Pallas kernels for 0%

profile of v2, /device:TPU:0, one launch (start us, length us, event | category | flops | bytes accessed | tf_op | source)
XLA Modules:
  0.0 215.3 jit_solution(12694843804109263434)
XLA Ops:
  7.2 0.0 copy-start
  7.2 0.1 add_remainder_fusion
  7.3 0.1 compare_and_fusion.1
  7.4 0.1 rem.52
  7.5 1.1 copy-done
  8.6 2.8 %gather_fusion = bf16[768,1024]{1,0:T(8,128)(2,1)S(1)} fusion(bf16[768,1024]{1,0:T(8,128)(2,1)S(1)} %copy-done, s32[1024]{0:T(1024)S(1)} %pad_clamp_fusion), kind=kCustom, calls=%fused_computation | custom fusion | bytes 3148800 | tf_op jit(solution)/shard_map/jit(_take)/gather | solution.py:17
  11.4 1.4 broadcast_select_fusion
  12.8 5.2 %all-to-all-start = ((bf16[8,96,1024]{2,1,0:T(8,128)(2,1)}), bf16[8,96,1024]{2,1,0:T(8,128)(2,1)S(1)}, u32[]{:S(2)}, u32[]{:S(2)}) async-start(bf16[8,96,1024]{2,1,0:T(8,128)(2,1)} %broadcast_select_fusion), calls=%async_computation | async-start | bytes 3145728 | tf_op jit(solution)/shard_map/all_to_all | solution.py:18
  18.0 0.0 all-reduce.2.cloned.1.call-start
  18.0 1.0 compare_and_fusion
  19.1 0.7 iota_compare_fusion
  19.9 19.1 %all-to-all-done = bf16[8,96,1024]{2,1,0:T(8,128)(2,1)S(1)} async-done(((bf16[8,96,1024]{2,1,0:T(8,128)(2,1)}), bf16[8,96,1024]{2,1,0:T(8,128)(2,1)S(1)}, u32[]{:S(2)}, u32[]{:S(2)}) %all-to-all-start) | async-done | bytes 1572896 | tf_op jit(solution)/shard_map/all_to_all | solution.py:18
  39.0 0.0 copy-start.2
  39.0 87.0 %gather_fusion.1 = bf16[20480,1024]{1,0:T(8,128)(2,1)} fusion(bf16[768,1024]{1,0:T(8,128)(2,1)S(1)} %bitcast.11, s32[20480]{0:T(1024)S(1)} %broadcast_clamp_fusion), kind=kCustom, calls=%fused_computation.1 | custom fusion | bytes 83968000 | tf_op jit(solution)/shard_map/jit(_take)/gather | solution.py:23
  125.9 0.0 copy-done.2
  125.9 0.0 copy-start.3
  125.9 0.0 copy-start.1
  125.9 29.3 %multiply_reduce_fusion = f32[40,512]{1,0:T(8,128)} fusion(f32[1024]{0:T(1024)S(1)} %copy-done.2, bf16[40,512,1024]{2,1,0:T(8,128)(2,1)} %bitcast.12, pred[40,512]{1,0:T(8,128)(4,1)S(1)} %get-tuple-element.2, bf16[40,512,512]{2,1,0:T(8,128)(2,1)} %param.9, pred[40,512]{1,0:T(8,128)(4,1)S(1)} %iota_compare_fusion), kind=kOutput, calls=%fused_computation.2 | convolution fusion | flops 21569187840 | bytes 63041536 | tf_op jit(solution)/shard_map/bps,bsk->bpk/dot_general | solution.py:27
  155.2 0.0 all-reduce.2.cloned.1.call-update
  155.3 33.8 %all-reduce.2.cloned.1.call-done = f32[40,512]{1,0:T(8,128)} async-done(((f32[40,512]{1,0:T(8,128)}), f32[40,512]{1,0:T(8,128)}) %all-reduce.2.cloned.1.call-update) | async-done | bytes 81936 | tf_op jit(solution)/shard_map/psum | solution.py:31
  189.0 7.9 %fusion.11 = f32[40,1,49]{2,1,0:T(1,128)S(1)} fusion(f32[40,49,512]{2,0,1:T(8,128)} %param.13, f32[40,512,1]{1,0,2:T(8,128)} %bitcast.16), kind=kOutput, calls=%fused_computation.10 | convolution fusion | flops 12042240 | bytes 4103840 | tf_op jit(solution)/shard_map/blp,bp->bl/dot_general | solution.py:32
  196.9 0.0 copy-done.3
  196.9 0.2 convolution_bitcast_fusion
  197.2 9.3 %all-gather.1 = f32[8,64,49]{1,2,0:T(8,128)S(1)} all-gather(f32[1,64,49]{1,2,0:T(8,128)S(1)} %convolution_bitcast_fusion), channel_id=2, replica_groups=mesh['row'=8,'col'=4] {'row'}, dimensions={0}, use_global_device_ids=true | all-gather | bytes 112896 | tf_op jit(solution)/shard_map/all_gather | solution.py:36
  206.4 0.6 reduce_sum.19
  207.1 1.3 constant_dynamic-slice_fusion
  208.4 0.0 copy-done.1
  (5 shorter events, 0.1 us)
Async XLA Ops:
  7.2 1.4 copy-start
  12.8 26.2 %all-to-all-start = ((bf16[8,96,1024]{2,1,0:T(8,128)(2,1)}), bf16[8,96,1024]{2,1,0:T(8,128)(2,1)S(1)}, u32[]{:S(2)}, u32[]{:S(2)}) async-start(bf16[8,96,1024]{2,1,0:T(8,128)(2,1)} %broadcast_select_fusion), calls=%async_computation | async-start | bytes 3145728 | tf_op jit(solution)/shard_map/all_to_all | solution.py:18
  18.0 171.1 %all-reduce.2.cloned.1.call-start = ((), (), s32[]{:S(2)}) async-start(), calls=%async_computation.1 | async-start | bytes 163840 | tf_op jit(solution)/shard_map/psum | solution.py:31
  39.0 87.0 %copy-start.2 = (f32[1024]{0:T(1024)S(1)}, f32[1024]{0:T(1024)}, u32[]{:S(2)}) copy-start(f32[1024]{0:T(1024)} %param.8) | copy-start | bytes 12292
  125.9 71.0 %copy-start.3 = (s32[40]{0:T(128)S(1)}, s32[40]{0:T(128)}, u32[]{:S(2)}) copy-start(s32[40]{0:T(128)} %param.12) | copy-start | bytes 484
  125.9 82.5 %copy-start.1 = (bf16[768,1024]{1,0:T(8,128)(2,1)S(1)}, bf16[768,1024]{1,0:T(8,128)(2,1)}, u32[]{:S(2)}) copy-start(bf16[768,1024]{1,0:T(8,128)(2,1)} %param.7) | copy-start | bytes 4718596
Sparse Core Ops, SparseCore 0:
  155.4 33.6 all-reduce.1
